TPU v7x, 1024 devices: a whole 4x4x32 slice. The times are simulated.
1024 devices in a mesh: section: 8 (over y, core), dp: 8 (over z_hi, x), mp: 16 (over z_lo).
Axes of the slice: x: 4, y: 4, z: 32 (z_hi: 2, z_lo: 16; z = z_hi * 16 + z_lo), core: 2. Of those that a mesh axis runs over, the one named last changes fastest.
Arguments:
- queries: bfloat16 [8, 3072, 4096], P('section', 'dp', 'mp'), may hold values from -200 to 200, as said below
- latents: bfloat16 [8, 512, 1280], P('dp', ('section', 'mp')), may hold values from -6 to 6
- key_weight: bfloat16 [8, 1280, 4096], P('section', None, 'mp'), may hold values from -0.15625 to 0.15625
- value_weight: bfloat16 [8, 1280, 4096], P('section', None, 'mp'), may hold values from -0.15625 to 0.15625
- out_weight: bfloat16 [8, 4096, 8192], P('section', 'mp'), may hold values from -0.375 to 0.375
- residual: bfloat16 [8, 3072, 8192], P('section', ('dp', 'mp')), may hold values from -3 to 3
- gate_angle: float32 [8], P('section'), may hold values from 0.3 to 1.2
- block_mask: int32 [8, 6, 8], P('dp'), may hold values from 0 to 1, as said below
Outputs:
- updated: bfloat16 [8, 3072, 8192], P('section', ('dp', 'mp'))
Inputs may be any that keep to these rules, and one draw needn't show every extreme that they name: `block_mask`: entries are 0 or 1; some whole blocks see no image. `queries`: rows may differ in scale from one another by a factor of up to 100.
All inputs are finite; a program needn't handle non-finite values.
Results may differ from a plain program's by a relative error of at most 0.019.
Values may be sent and summed in bfloat16 or wider, within the bound.
A program may use at most 32 MiB of HBM per device.

v0:
```python
import jax
import jax.numpy as jnp
from jax import lax
from jax.sharding import PartitionSpec as P

HEAD_DIM = 128


def joined_along(blocks, dim):
    blocks = jnp.moveaxis(blocks, 0, dim)
    lengths = blocks.shape
    return blocks.reshape(*lengths[:dim], lengths[dim] * lengths[dim + 1], *lengths[dim + 2 :])


def from_everyone(x, axis):
    count = lax.axis_size(axis)
    return lax.all_to_all(jnp.broadcast_to(x[None], (count, *x.shape)), axis, 0, 0, tiled=True)


def gather_directly(x, axis, dim):
    return joined_along(from_everyone(x, axis), dim)


def token_mask(mask_table):
    blocks, images = mask_table.shape
    spread = jnp.broadcast_to(mask_table[:, None, :, None], (blocks, 64, images, 64))
    return spread.reshape(blocks * 64, images * 64) > 0


def attend(query_rows, key_rows, value_rows, allowed_rows):
    length = query_rows.shape[0]
    key_count = key_rows.shape[0]
    heads_here = query_rows.shape[1] // HEAD_DIM
    query_heads = query_rows.reshape(length, heads_here, HEAD_DIM)
    key_heads = key_rows.reshape(key_count, heads_here, HEAD_DIM)
    value_heads = value_rows.reshape(key_count, heads_here, HEAD_DIM)
    scores = jnp.einsum(
        "thd,khd->htk", query_heads, key_heads, preferred_element_type=jnp.float32
    ) * HEAD_DIM ** (-0.5)
    allowed = allowed_rows[None]
    masked = jnp.where(allowed, scores, -1e30)
    row_max = jnp.max(masked, axis=-1, keepdims=True)
    any_live = jnp.any(allowed, axis=-1, keepdims=True)
    row_max = jnp.where(any_live, row_max, 0.0)
    numerators = jnp.exp(masked - row_max)
    denominator = jnp.maximum(jnp.sum(numerators, axis=-1, keepdims=True), 1.0)
    weights = (numerators / denominator).astype(jnp.bfloat16)
    attended = jnp.einsum("htk,khd->thd", weights, value_heads, preferred_element_type=jnp.float32)
    return attended.reshape(length, heads_here * HEAD_DIM).astype(jnp.bfloat16)


def local(queries, latents, key_weight, value_weight, out_weight, residual, gate_angle, block_mask):
    key_proj = key_weight[0]
    value_proj = value_weight[0]
    head_width = key_proj.shape[1]
    local_rows = gather_directly(latents, "mp", 1)
    flat_rows = gather_directly(local_rows, "section", 1)[0]
    key_part = jnp.dot(flat_rows, key_proj, preferred_element_type=jnp.float32).astype(jnp.bfloat16)
    value_part = jnp.dot(flat_rows, value_proj, preferred_element_type=jnp.float32).astype(
        jnp.bfloat16
    )
    projected = jnp.concatenate([key_part, value_part], axis=1)[None]
    key_rows = projected[0][:, :head_width]
    value_rows = projected[0][:, head_width:]
    query_rows = queries[0]
    allowed_all = token_mask(block_mask[0])
    out_proj = out_weight[0]
    gate_factor = jnp.tanh(gate_angle[0])
    attended = attend(query_rows, key_rows, value_rows, allowed_all)
    partial_value = jnp.dot(attended, out_proj, preferred_element_type=jnp.float32)
    summed = lax.psum_scatter(
        partial_value.astype(jnp.bfloat16), "mp", scatter_dimension=0, tiled=True
    ).astype(jnp.float32)
    updated = (residual[0].astype(jnp.float32) + gate_factor * summed).astype(jnp.bfloat16)
    return updated[None]


def solution(mesh):
    return jax.shard_map(
        local,
        mesh=mesh,
        in_specs=(
            P("section", "dp", "mp"),
            P("dp", ("section", "mp"), None),
            P("section", None, "mp"),
            P("section", None, "mp"),
            P("section", "mp", None),
            P("section", ("dp", "mp"), None),
            P("section"),
            P("dp", None, None),
        ),
        out_specs=P("section", ("dp", "mp"), None),
        check_vma=False,
    )
```

profile of v0, /device:TPU:14, one launch (start us, length us, event | category | flops | bytes accessed | tf_op | source)
XLA Modules:
  0.0 314.4 jit_solution(505602335723407619)
XLA Ops:
  6.5 0.0 copy-start
  6.5 0.8 broadcast_in_dim.54
  7.4 50.3 %all_to_all.10 = bf16[16,1,4,1280]{3,2,1,0:T(4,128)(2,1)S(1)} all-to-all(bf16[16,1,4,1280]{3,2,1,0:T(4,128)(2,1)S(1)} %broadcast_in_dim.54), channel_id=1, replica_groups=mesh['section'=8,'dp'=8,'mp'=16] {'mp'}, dimensions={0} | all-to-all | bytes 327680 | tf_op jit(solution)/shard_map/all_to_all | solution.py:17
  57.7 1.2 broadcast_in_dim.56
  58.9 0.0 copy-start.4
  58.9 0.0 copy-start.3
  58.9 5.0 %all-to-all-start.1 = ((bf16[8,1,64,1280]{3,2,1,0:T(8,128)(2,1)}), bf16[8,1,64,1280]{3,2,1,0:T(8,128)(2,1)S(1)}, u32[]{:S(2)}, u32[]{:S(2)}) async-start(bf16[8,1,64,1280]{3,2,1,0:T(8,128)(2,1)} %broadcast_in_dim.56), calls=%async_computation.1 | async-start | bytes 2621440 | tf_op jit(solution)/shard_map/all_to_all | solution.py:17
  63.9 0.0 reduce-scatter.2.cloned.1.call-start
  63.9 0.0 copy-done.4
  63.9 0.2 broadcast_in_dim.57
  64.1 0.5 gt.23
  64.6 0.3 copy.15
  65.0 0.0 copy-done.3
  65.0 0.1 reshape_squeeze.3
  65.0 6.9 %broadcast_reduce_fusion = pred[6,64]{1,0:T(8,128)(4,1)S(1)} fusion(pred[6,8]{1,0:T(8,128)(4,1)S(1)} %fusion.7), kind=kLoop, calls=%fused_computation.11 | loop fusion | flops 196224 | bytes 432 | tf_op jit(solution)/shard_map/reduce_or | solution.py:43
  72.0 0.1 broadcast_in_dim.60
  72.1 9.1 %all-to-all-done.1 = bf16[8,1,64,1280]{3,2,1,0:T(8,128)(2,1)S(1)} async-done(((bf16[8,1,64,1280]{3,2,1,0:T(8,128)(2,1)}), bf16[8,1,64,1280]{3,2,1,0:T(8,128)(2,1)S(1)}, u32[]{:S(2)}, u32[]{:S(2)}) %all-to-all-start.1) | async-done | bytes 1310752 | tf_op jit(solution)/shard_map/all_to_all | solution.py:17
  81.2 0.0 copy-done
  81.2 0.5 convolution_convert_fusion.1
  81.8 0.0 copy-start.5
  81.8 0.5 fusion.8
  82.3 0.2 fusion.1
  82.6 0.3 copy-done.5
  82.9 0.6 convolution_convert_fusion.2
  83.4 0.0 copy-start.1
  83.4 0.4 convolution_convert_fusion.3
  83.8 1.8 copy-done.1
  85.6 4.5 %convolution_convert_fusion = bf16[384,8192]{1,0:T(8,128)(2,1)} fusion(bf16[384,256]{0,1:T(8,128)(2,1)S(1)} %bitcast.35, bf16[1,256,8192]{2,1,0:T(8,128)(2,1)S(1)} %copy-done.1), kind=kOutput, calls=%fused_computation | convolution fusion | flops 1613758464 | bytes 10682368 | tf_op jit(solution)/shard_map/dot_general | solution.py:70
  90.1 0.0 reduce-scatter.2.cloned.1.call-update
  90.9 214.8 %reduce-scatter.2.cloned.1.call-done = bf16[24,8192]{1,0:T(8,128)(2,1)} async-done(((bf16[384,8192]{1,0:T(8,128)(2,1)}), bf16[24,8192]{1,0:T(8,128)(2,1)}) %reduce-scatter.2.cloned.1.call-update) | async-done | bytes 393232 | tf_op jit(solution)/shard_map/reduce_scatter | solution.py:71
  305.7 0.0 copy-done.2
  305.7 1.9 fusion.5
  (5 shorter events, 0.1 us)
Async XLA Ops:
  6.5 74.7 %copy-start = (bf16[1,1280,256]{2,1,0:T(8,128)(2,1)S(1)}, bf16[1,1280,256]{2,1,0:T(8,128)(2,1)}, u32[]{:S(2)}) copy-start(bf16[1,1280,256]{2,1,0:T(8,128)(2,1)} %param.10) | copy-start | bytes 1966084
  58.9 5.1 %copy-start.4 = (s32[1,6,8]{2,0,1:T(1,128)S(1)}, s32[1,6,8]{2,0,1:T(1,128)}, u32[]{:S(2)}) copy-start(s32[1,6,8]{2,0,1:T(1,128)} %param.15) | copy-start | bytes 580
  58.9 6.1 %copy-start.3 = (bf16[1,384,256]{2,1,0:T(8,128)(2,1)S(1)}, bf16[1,384,256]{2,1,0:T(8,128)(2,1)}, u32[]{:S(2)}) copy-start(bf16[1,384,256]{2,1,0:T(8,128)(2,1)} %param.8) | copy-start | bytes 589828
  58.9 22.3 %all-to-all-start.1 = ((bf16[8,1,64,1280]{3,2,1,0:T(8,128)(2,1)}), bf16[8,1,64,1280]{3,2,1,0:T(8,128)(2,1)S(1)}, u32[]{:S(2)}, u32[]{:S(2)}) async-start(bf16[8,1,64,1280]{3,2,1,0:T(8,128)(2,1)} %broadcast_in_dim.56), calls=%async_computation.1 | async-start | bytes 2621440 | tf_op jit(solution)/shard_map/all_to_all | solution.py:17
  63.9 241.8 %reduce-scatter.2.cloned.1.call-start = ((), (), s32[]{:S(2)}) async-start(), calls=%async_computation.3 | async-start | bytes 6684672 | tf_op jit(solution)/shard_map/reduce_scatter | solution.py:71
  81.8 1.1 copy-start.5
  83.4 2.2 copy-start.1
  90.1 215.6 %copy-start.2 = (bf16[1,24,8192]{2,1,0:T(8,128)(2,1)S(1)}, bf16[1,24,8192]{2,1,0:T(8,128)(2,1)}, u32[]{:S(2)}) copy-start(bf16[1,24,8192]{2,1,0:T(8,128)(2,1)} %param.13) | copy-start | bytes 1179652
Sparse Core Ops, SparseCore 0:
  90.2 215.3 reduce-scatter.1
where the time goes:
time: 315 us; the launch traced here: 314 us
  waiting for transfers between devices  224 us (71%)
  blocking collectives  50.3 us (16%)
  between operations  14.2 us (5%)
  other arithmetic  9.05 us (3%)
  matrix products  6.52 us (2%)
  local copies, waits for them, and re-layouts  5.27 us (2%)
  starting transfers between devices  5.05 us (2%)
    reduce_scatter x1, waiting for transfers between devices, local(): lax.psum_scatter(partial_value.astype(jnp.bfloat16), 'mp', scatter_dimens...  215 us
    all_to_all x1, blocking collectives, from_everyone(): lax.all_to_all(jnp.broadcast_to(x[None], (count, *x.shape)), axis, 0, 0,...  50.3 us
    all_to_all x1, waiting for transfers between devices, from_everyone(): lax.all_to_all(jnp.broadcast_to(x[None], (count, *x.shape)), axis, 0, 0,...  9.14 us
    reduce_or x1, other arithmetic, attend(): any_live = jnp.any(allowed, axis=-1, keepdims=True)  6.94 us
  transfers between devices with their start and end apart: 2, of which 2 were waited for; matrix products, arithmetic and copies ran while one was open for 3% of the time, Pallas kernels for 0%

commit v1 on v0

--- a/solution.py
+++ b/solution.py
@@ -1,9 +1,16 @@
+import functools
+
 import jax
 import jax.numpy as jnp
 from jax import lax
+from jax.experimental import pallas as pl
+from jax.experimental.pallas import tpu as pltpu
 from jax.sharding import PartitionSpec as P
 
 HEAD_DIM = 128
+CHUNKS = 4
+TILE = 512
+MESH = pl.DeviceIdType.MESH
 
 
 def joined_along(blocks, dim):
@@ -49,29 +56,159 @@
     return attended.reshape(length, heads_here * HEAD_DIM).astype(jnp.bfloat16)
 
 
+def ring_place(n_mp):
+    columns = lax.axis_size("dp") // 2
+    half = lax.axis_index("dp") // columns
+    column = lax.axis_index("dp") % columns
+    return half * n_mp + lax.axis_index("mp"), column, columns
+
+
+def ring_device(place, n_mp, column, columns):
+    place = place % (2 * n_mp)
+    return {"dp": (place // n_mp) * columns + column, "mp": place % n_mp}
+
+
+def sum_kernel(
+    n_mp, att_ref, w_ref, res_ref, gate_ref, out_ref,
+    part, from_left, from_right, right_send, left_send, right_recv, left_recv,
+):
+    place, column, columns = ring_place(n_mp)
+    me = lax.axis_index("mp")
+    right = ring_device(place + 1, n_mp, column, columns)
+    left = ring_device(place + 2 * n_mp - 1, n_mp, column, columns)
+    far = n_mp // 2
+    rows = out_ref.shape[0]
+    width = w_ref.shape[1] // CHUNKS
+
+    barrier = pltpu.get_barrier_semaphore()
+    pl.semaphore_signal(barrier, inc=1, device_id=left, device_id_type=MESH)
+    pl.semaphore_signal(barrier, inc=1, device_id=right, device_id_type=MESH)
+
+    def to_right(step, c):
+        block = (me + far - step + n_mp) % n_mp
+        return pltpu.make_async_remote_copy(
+            src_ref=part.at[c, block], dst_ref=from_left.at[step, c],
+            send_sem=right_send.at[step, c], recv_sem=right_recv.at[step, c],
+            device_id=right, device_id_type=MESH,
+        )
+
+    def to_left(step, c):
+        block = (me - far + 1 + step + n_mp) % n_mp
+        return pltpu.make_async_remote_copy(
+            src_ref=part.at[c, block], dst_ref=from_right.at[step, c],
+            send_sem=left_send.at[step, c], recv_sem=left_recv.at[step, c],
+            device_id=left, device_id_type=MESH,
+        )
+
+    for c in range(CHUNKS):
+        @pl.loop(0, width // TILE)
+        def _(tile):
+            columns_in = pl.ds(pl.multiple_of(c * width + tile * TILE, TILE), TILE)
+            columns_out = pl.ds(pl.multiple_of(tile * TILE, TILE), TILE)
+            term = jnp.dot(att_ref[...], w_ref[:, columns_in], preferred_element_type=jnp.float32)
+            part[c, :, :, columns_out] = term.reshape(n_mp, rows, TILE).astype(jnp.bfloat16)
+
+        if c == 0:
+            pl.semaphore_wait(barrier, 2)
+        to_right(0, c).start()
+        to_left(0, c).start()
+
+    def add_right(step, c):
+        to_right(step - 1, c).wait_recv()
+        block = (me + far - step + n_mp) % n_mp
+        part[c, block] = (
+            part[c, block].astype(jnp.float32) + from_left[step - 1, c].astype(jnp.float32)
+        ).astype(jnp.bfloat16)
+        to_right(step, c).start()
+
+    def add_left(step, c):
+        to_left(step - 1, c).wait_recv()
+        block = (me - far + 1 + step + n_mp) % n_mp
+        part[c, block] = (
+            part[c, block].astype(jnp.float32) + from_right[step - 1, c].astype(jnp.float32)
+        ).astype(jnp.bfloat16)
+        to_left(step, c).start()
+
+    @pl.loop(1, far - 1)
+    def _(step):
+        for c in range(CHUNKS):
+            add_right(step, c)
+            add_left(step, c)
+
+    gate = jnp.tanh(gate_ref[...])
+    for c in range(CHUNKS):
+        add_right(far - 1, c)
+    for c in range(CHUNKS):
+        to_left(far - 2, c).wait_recv()
+        to_right(far - 1, c).wait_recv()
+        here = pl.ds(c * width, width)
+        branch = (
+            part[c, me].astype(jnp.float32)
+            + from_left[far - 1, c].astype(jnp.float32)
+            + from_right[far - 2, c].astype(jnp.float32)
+        )
+        out_ref[:, here] = (res_ref[:, here].astype(jnp.float32) + gate * branch).astype(jnp.bfloat16)
+
+    @pl.loop(0, far - 1)
+    def _(step):
+        for c in range(CHUNKS):
+            to_right(step, c).wait_send()
+            to_left(step, c).wait_send()
+
+    for c in range(CHUNKS):
+        to_right(far - 1, c).wait_send()
+
+
+def summed_branch(attended, out_proj, residual, gate):
+    n_mp = lax.axis_size("mp")
+    rows, wide = residual.shape
+    far = n_mp // 2
+    width = wide // CHUNKS
+    return pl.pallas_call(
+        functools.partial(sum_kernel, n_mp),
+        out_shape=jax.ShapeDtypeStruct((rows, wide), jnp.bfloat16),
+        in_specs=[pl.BlockSpec(memory_space=pltpu.VMEM)] * 4,
+        out_specs=pl.BlockSpec(memory_space=pltpu.VMEM),
+        scratch_shapes=[
+            pltpu.VMEM((CHUNKS, n_mp, rows, width), jnp.bfloat16),
+            pltpu.VMEM((far, CHUNKS, rows, width), jnp.bfloat16),
+            pltpu.VMEM((far - 1, CHUNKS, rows, width), jnp.bfloat16),
+            pltpu.SemaphoreType.DMA((far, CHUNKS)),
+            pltpu.SemaphoreType.DMA((far - 1, CHUNKS)),
+            pltpu.SemaphoreType.DMA((far, CHUNKS)),
+            pltpu.SemaphoreType.DMA((far - 1, CHUNKS)),
+        ],
+        compiler_params=pltpu.CompilerParams(
+            collective_id=0, has_side_effects=True, vmem_limit_bytes=60 * 2**20
+        ),
+        name="ring_sum",
+    )(attended, out_proj, residual, gate)
+
+
+def window_rows(attended):
+    n_mp = lax.axis_size("mp")
+    n_dp = lax.axis_size("dp")
+    me = lax.axis_index("mp")
+    length = attended.shape[0]
+    upper = lax.slice_in_dim(attended, length // 2, length, axis=0)
+    lower = lax.slice_in_dim(attended, 0, length // 2, axis=0)
+    sent = jnp.where(me < n_mp // 2, upper, lower)
+    pairs = [(d, (d + n_dp // 2) % n_dp) for d in range(n_dp)]
+    came = lax.ppermute(sent, "dp", pairs)
+    other = jnp.concatenate([came, came], axis=0)
+    offset = jnp.arange(length) // (length // n_mp) - me
+    own = (offset > -(n_mp // 2)) & (offset <= n_mp // 2)
+    return jnp.where(own[:, None], attended, other)
+
+
 def local(queries, latents, key_weight, value_weight, out_weight, residual, gate_angle, block_mask):
-    key_proj = key_weight[0]
-    value_proj = value_weight[0]
-    head_width = key_proj.shape[1]
     local_rows = gather_directly(latents, "mp", 1)
     flat_rows = gather_directly(local_rows, "section", 1)[0]
-    key_part = jnp.dot(flat_rows, key_proj, preferred_element_type=jnp.float32).astype(jnp.bfloat16)
-    value_part = jnp.dot(flat_rows, value_proj, preferred_element_type=jnp.float32).astype(
-        jnp.bfloat16
-    )
-    projected = jnp.concatenate([key_part, value_part], axis=1)[None]
-    key_rows = projected[0][:, :head_width]
-    value_rows = projected[0][:, head_width:]
-    query_rows = queries[0]
-    allowed_all = token_mask(block_mask[0])
-    out_proj = out_weight[0]
-    gate_factor = jnp.tanh(gate_angle[0])
-    attended = attend(query_rows, key_rows, value_rows, allowed_all)
-    partial_value = jnp.dot(attended, out_proj, preferred_element_type=jnp.float32)
-    summed = lax.psum_scatter(
-        partial_value.astype(jnp.bfloat16), "mp", scatter_dimension=0, tiled=True
-    ).astype(jnp.float32)
-    updated = (residual[0].astype(jnp.float32) + gate_factor * summed).astype(jnp.bfloat16)
+    key_rows = jnp.dot(flat_rows, key_weight[0], preferred_element_type=jnp.float32).astype(jnp.bfloat16)
+    value_rows = jnp.dot(flat_rows, value_weight[0], preferred_element_type=jnp.float32).astype(jnp.bfloat16)
+    attended = attend(queries[0], key_rows, value_rows, token_mask(block_mask[0]))
+    gate = jnp.broadcast_to(gate_angle.reshape(1, 1), (1, 128))[:, :1]
+    updated = summed_branch(window_rows(attended), out_weight[0], residual[0], gate)
     return updated[None]
 
 

time: 315 us -> 195 us (0.62)
  the two profiles are of different devices: /device:TPU:14 before, /device:TPU:1 now
where the time goes in v1:
time: 195 us; the launch traced here: 194 us
  Pallas kernels  75.3 us (39%)
  blocking collectives  49.3 us (25%)
  waiting for transfers between devices  35 us (18%)
  starting transfers between devices  18.7 us (10%)
  other arithmetic  8.12 us (4%)
  local copies, waits for them, and re-layouts  5.19 us (3%)
  matrix products  2.03 us (1%)
    pallas_call x1, Pallas kernels, summed_branch(): pl.pallas_call(functools.partial(sum_kernel, n_mp), out_shape=jax.ShapeDt...  75.3 us
    all_to_all x1, blocking collectives, from_everyone(): lax.all_to_all(jnp.broadcast_to(x[None], (count, *x.shape)), axis, 0, 0,...  49.3 us
    ppermute x1, waiting for transfers between devices, window_rows(): came = lax.ppermute(sent, 'dp', pairs)  26.1 us
    ppermute x1, starting transfers between devices, window_rows(): came = lax.ppermute(sent, 'dp', pairs)  11.6 us
    all_to_all x1, waiting for transfers between devices, from_everyone(): lax.all_to_all(jnp.broadcast_to(x[None], (count, *x.shape)), axis, 0, 0,...  8.96 us
    all_to_all x1, starting transfers between devices, from_everyone(): lax.all_to_all(jnp.broadcast_to(x[None], (count, *x.shape)), axis, 0, 0,...  7.1 us
    reduce_or x1, other arithmetic, attend(): any_live = jnp.any(allowed, axis=-1, keepdims=True)  6.95 us
  transfers between devices with their start and end apart: 2, of which 2 were waited for; matrix products, arithmetic and copies ran while one was open for 4% of the time, Pallas kernels for 0%

profile of v1, /device:TPU:1, one launch (start us, length us, event | category | flops | bytes accessed | tf_op | source)
XLA Modules:
  0.0 194.5 jit_solution(2922887504140020609)
XLA Ops:
  0.0 0.0 copy-start
  0.0 0.8 broadcast_in_dim.67
  0.8 49.3 %all_to_all.10 = bf16[16,1,4,1280]{3,2,1,0:T(4,128)(2,1)S(1)} all-to-all(bf16[16,1,4,1280]{3,2,1,0:T(4,128)(2,1)S(1)} %broadcast_in_dim.67), channel_id=1, replica_groups=mesh['section'=8,'dp'=8,'mp'=16] {'mp'}, dimensions={0} | all-to-all | bytes 327680 | tf_op jit(solution)/shard_map/all_to_all | solution.py:24
  50.2 1.1 broadcast_in_dim.69
  51.3 0.0 copy-start.1
  51.3 0.0 copy-start.2
  51.3 7.1 %all-to-all-start.1 = ((bf16[8,1,64,1280]{3,2,1,0:T(8,128)(2,1)}), bf16[8,1,64,1280]{3,2,1,0:T(8,128)(2,1)S(1)}, u32[]{:S(2)}, u32[]{:S(2)}) async-start(bf16[8,1,64,1280]{3,2,1,0:T(8,128)(2,1)} %broadcast_in_dim.69), calls=%async_computation.1 | async-start | bytes 2621440 | tf_op jit(solution)/shard_map/all_to_all | solution.py:24
  58.4 0.0 copy-done.1
  58.4 0.1 reshape_squeeze.3
  58.5 0.0 copy-done.2
  58.5 0.2 broadcast_in_dim.70
  58.7 0.0 copy-start.3
  58.7 0.5 gt.35
  59.2 0.3 copy.17
  59.5 6.9 %broadcast_reduce_fusion = pred[6,64]{1,0:T(8,128)(4,1)S(1)} fusion(pred[6,8]{1,0:T(8,128)(4,1)S(1)} %fusion.4), kind=kLoop, calls=%fused_computation.7 | loop fusion | flops 196224 | bytes 432 | tf_op jit(solution)/shard_map/reduce_or | solution.py:50
  66.5 0.1 broadcast_in_dim.73
  67.2 9.0 %all-to-all-done.1 = bf16[8,1,64,1280]{3,2,1,0:T(8,128)(2,1)S(1)} async-done(((bf16[8,1,64,1280]{3,2,1,0:T(8,128)(2,1)}), bf16[8,1,64,1280]{3,2,1,0:T(8,128)(2,1)S(1)}, u32[]{:S(2)}, u32[]{:S(2)}) %all-to-all-start.1) | async-done | bytes 1310752 | tf_op jit(solution)/shard_map/all_to_all | solution.py:24
  76.2 0.0 copy-done
  76.2 0.5 convolution_convert_fusion.1
  76.8 0.0 copy-done.3
  76.8 0.6 convolution_convert_fusion
  77.3 0.5 fusion.9
  77.9 0.2 fusion
  78.1 0.4 convolution_convert_fusion.2
  78.5 0.1 slice_select_fusion
  78.6 0.1 copy.26
  78.7 11.6 %collective-permute-start = (bf16[192,256]{1,0:T(8,128)(2,1)S(1)}, bf16[192,256]{1,0:T(8,128)(2,1)S(1)}, u32[]{:S(2)}, u32[]{:S(2)}) collective-permute-start(bf16[192,256]{1,0:T(8,128)(2,1)S(1)} %copy.26), channel_id=1, source_target_pairs={{0,64},{16,80},{32,96},{48,112},{64,0},{80,16},{96,32},{112,48},{1... | collective-permute-start | bytes 294920 | tf_op jit(solution)/shard_map/ppermute | solution.py:197
  90.3 0.1 copy.25
  90.5 26.1 %collective-permute-done = bf16[192,256]{1,0:T(8,128)(2,1)S(1)} collective-permute-done((bf16[192,256]{1,0:T(8,128)(2,1)S(1)}, bf16[192,256]{1,0:T(8,128)(2,1)S(1)}, u32[]{:S(2)}, u32[]{:S(2)}) %collective-permute-start) | collective-permute-done | bytes 98336 | tf_op jit(solution)/shard_map/ppermute | solution.py:197
  116.6 0.8 maximum_select_fusion.att_ref
  117.4 75.3 %ring_sum.1 = bf16[24,8192]{1,0:T(8,128)(2,1)} custom-call(bf16[384,256]{1,0:T(8,128)(2,1)} %maximum_select_fusion.att_ref, bf16[256,8192]{1,0:T(8,128)(2,1)} %bitcast.29, bf16[24,8192]{1,0:T(8,128)(2,1)} %bitcast.36, f32[1,1]{1,0:T(1,128)} %bitcast.28.gate_ref), custom_call_target="tpu_custom_call" | custom-call | tf_op jit(solution)/shard_map/ring_sum/pallas_call | solution.py:167
  192.7 1.8 copy.36
  (5 shorter events, 0.1 us)
Async XLA Ops:
  0.0 76.2 %copy-start = (bf16[1,1280,256]{2,1,0:T(8,128)(2,1)S(1)}, bf16[1,1280,256]{2,1,0:T(8,128)(2,1)}, u32[]{:S(2)}) copy-start(bf16[1,1280,256]{2,1,0:T(8,128)(2,1)} %param.11) | copy-start | bytes 1966084
  51.3 7.1 %copy-start.1 = (bf16[1,384,256]{2,1,0:T(8,128)(2,1)S(1)}, bf16[1,384,256]{2,1,0:T(8,128)(2,1)}, u32[]{:S(2)}) copy-start(bf16[1,384,256]{2,1,0:T(8,128)(2,1)} %param.8) | copy-start | bytes 589828
  51.3 7.2 %copy-start.2 = (s32[1,6,8]{2,0,1:T(1,128)S(1)}, s32[1,6,8]{2,0,1:T(1,128)}, u32[]{:S(2)}) copy-start(s32[1,6,8]{2,0,1:T(1,128)} %param.15) | copy-start | bytes 580
  51.3 24.9 %all-to-all-start.1 = ((bf16[8,1,64,1280]{3,2,1,0:T(8,128)(2,1)}), bf16[8,1,64,1280]{3,2,1,0:T(8,128)(2,1)S(1)}, u32[]{:S(2)}, u32[]{:S(2)}) async-start(bf16[8,1,64,1280]{3,2,1,0:T(8,128)(2,1)} %broadcast_in_dim.69), calls=%async_computation.1 | async-start | bytes 2621440 | tf_op jit(solution)/shard_map/all_to_all | solution.py:24
  58.7 18.1 %copy-start.3 = (bf16[1,1280,256]{2,1,0:T(8,128)(2,1)S(1)}, bf16[1,1280,256]{2,1,0:T(8,128)(2,1)}, u32[]{:S(2)}) copy-start(bf16[1,1280,256]{2,1,0:T(8,128)(2,1)} %param.10) | copy-start | bytes 1966084
  78.7 37.8 %collective-permute-start = (bf16[192,256]{1,0:T(8,128)(2,1)S(1)}, bf16[192,256]{1,0:T(8,128)(2,1)S(1)}, u32[]{:S(2)}, u32[]{:S(2)}) collective-permute-start(bf16[192,256]{1,0:T(8,128)(2,1)S(1)} %copy.26), channel_id=1, source_target_pairs={{0,64},{16,80},{32,96},{48,112},{64,0},{80,16},{96,32},{112,48},{1... | collective-permute-start | bytes 294920 | tf_op jit(solution)/shard_map/ppermute | solution.py:197
